TPU v7x, 256 devices: a whole 4x4x8 slice. The times are simulated.
256 devices in a mesh: row: 32 (over z, y), col: 8 (over x, core).
Axes of the slice: x: 4, y: 4, z: 8, core: 2. Of those that a mesh axis runs over, the one named last changes fastest.
Arguments:
- inputs: bfloat16 [1024, 12288], P('row', 'col'), may hold values from -6 to 6
- hidden_pre: bfloat16 [1024, 24576], P(None, 'row'), may hold values from -8 to 8
- out_grad: bfloat16 [1024, 12288], P('row', 'col'), may hold values from -6 to 6
- weight_in: bfloat16 [12288, 24576], P('col', 'row'), may hold values from -0.0546875 to 0.0546875
- weight_out: bfloat16 [24576, 12288], P('row', 'col'), may hold values from -0.0390625 to 0.0390625
Outputs:
- grad_in: bfloat16 [1024, 12288], P('row', 'col')
- grad_weight_in: bfloat16 [12288, 24576], P('col', 'row')
- grad_weight_out: bfloat16 [24576, 12288], P('row', 'col')
All inputs are finite; a program needn't handle non-finite values.
Results may differ from a plain program's by a relative error of at most 0.0049.
Values may be sent and summed in bfloat16 or wider, within the bound.
A program may use at most 128 MiB of HBM per device.

v0:
```python
import jax
import jax.numpy as jnp
from jax import lax
from jax.sharding import PartitionSpec as P


def gelu_parts(hidden_pre):
    hval = hidden_pre.astype(jnp.float32)
    inner = 0.7978845608 * (hval + 0.044715 * hval * hval * hval)
    tval = jnp.tanh(inner)
    act = 0.5 * hval * (1.0 + tval)
    slope = 0.5 * (1.0 + tval) + 0.5 * hval * (1.0 - tval * tval) * 0.7978845608 * (
        1.0 + 3.0 * 0.044715 * hval * hval
    )
    return (act, slope)


def contract_rows(left, right):
    return lax.dot_general(
        left, right, (((0,), (0,)), ((), ())), preferred_element_type=jnp.float32
    )


def contract_cols(left, right):
    return lax.dot_general(
        left, right, (((1,), (1,)), ((), ())), preferred_element_type=jnp.float32
    )


def body(inputs, hidden_pre, out_grad, weight_in, weight_out):
    act, slope = gelu_parts(hidden_pre)
    act_b = act.astype(jnp.bfloat16)
    grad_all, input_all = (
        lax.all_gather(out_grad, "row", axis=0, tiled=True),
        lax.all_gather(inputs, "row", axis=0, tiled=True),
    )
    grad_weight_out = contract_rows(act_b, grad_all).astype(jnp.bfloat16)
    col_rows = grad_all.shape[0] // lax.axis_size("col")
    piece = grad_all
    d_act = lax.psum_scatter(
        contract_cols(piece, weight_out), "col", scatter_dimension=0, tiled=True
    )
    slope_mine = lax.dynamic_slice_in_dim(slope, lax.axis_index("col") * col_rows, col_rows, 0)
    d_mine = (d_act * slope_mine).astype(jnp.bfloat16)
    d_hid = lax.all_gather(d_mine, "col", axis=0, tiled=True)
    piece = d_hid
    grad_in = lax.psum_scatter(
        contract_cols(piece, weight_in), "row", scatter_dimension=0, tiled=True
    ).astype(jnp.bfloat16)
    grad_weight_in = contract_rows(input_all, d_hid).astype(jnp.bfloat16)
    return (grad_in, grad_weight_in, grad_weight_out)


def solution(mesh):
    return jax.shard_map(
        body,
        mesh=mesh,
        in_specs=(
            P("row", "col"),
            P(None, "row"),
            P("row", "col"),
            P("col", "row"),
            P("row", "col"),
        ),
        out_specs=(P("row", "col"), P("col", "row"), P("row", "col")),
        check_vma=False,
    )
```

profile of v0, /device:TPU:2, one launch (start us, length us, event | category | flops | bytes accessed | tf_op | source)
XLA Modules:
  0.0 481.1 jit_solution(16308524493274345741)
XLA Ops:
  7.2 0.0 copy-start
  7.2 0.0 all-gather.4.cloned.1.call-start
  7.2 0.7 all-gather.4.cloned.1.call-update
  7.9 0.0 reduce-scatter.3.cloned.1.call-start
  8.0 85.1 %all-gather.4.cloned.1.call-done = bf16[1024,1536]{1,0:T(8,128)(2,1)} async-done(((bf16[32,1536]{1,0:T(8,128)(2,1)}), bf16[1024,1536]{1,0:T(8,128)(2,1)}) %all-gather.4.cloned.1.call-update) | async-done | bytes 3145744 | tf_op jit(solution)/shard_map/all_gather | solution.py:34
  93.0 6.9 %fusion.12 = f32[1024,768]{1,0:T(8,128)} fusion(bf16[1024,1536]{1,0:T(8,128)(2,1)} %all-gather.4.cloned.1.call-done, bf16[768,1536]{1,0:T(8,128)(2,1)} %param.9), kind=kOutput, calls=%fused_computation.21 | convolution fusion | flops 2415919104 | bytes 8650752 | tf_op jit(solution)/shard_map/dot_general | solution.py:25
  99.9 0.0 reduce-scatter.3.cloned.1.call-update
  99.9 0.0 all-gather.6.cloned.1.call-start
  100.0 3.3 convert_element_type.21
  103.3 6.0 %fusion.1 = (f32[1024,768]{1,0:T(8,128)}, f32[1024,768]{1,0:T(8,128)}, f32[1024,768]{1,0:T(8,128)}) fusion(bf16[1024,768]{1,0:T(8,128)(2,1)} %param.6), kind=kLoop, calls=%fused_computation.4 | loop fusion | flops 6291456 | bytes 11010048 | tf_op jit(solution)/shard_map/tanh | solution.py:10
  109.2 22.6 %reduce-scatter.3.cloned.1.call-done = f32[128,768]{1,0:T(8,128)} async-done(((f32[1024,768]{1,0:T(8,128)}), f32[128,768]{1,0:T(8,128)}) %reduce-scatter.3.cloned.1.call-update) | async-done | bytes 393232 | tf_op jit(solution)/shard_map/reduce_scatter | solution.py:40
  131.9 2.3 fusion.7
  134.2 0.0 all-gather.6.cloned.1.call-update
  134.2 0.0 all-gather.8.cloned.1.call-start
  134.3 0.5 all-gather.8.cloned.1.call-update
  134.8 0.0 reduce-scatter.5.cloned.1.call-start
  134.8 27.0 %all-gather.6.cloned.1.call-done = bf16[1024,768]{1,0:T(8,128)(2,1)} async-done(((bf16[128,768]{1,0:T(8,128)(2,1)}), bf16[1024,768]{1,0:T(8,128)(2,1)}) %all-gather.6.cloned.1.call-update) | async-done | bytes 1572880 | tf_op jit(solution)/shard_map/all_gather | solution.py:45
  161.8 0.0 copy-done
  161.8 6.0 %fusion.13 = f32[1024,1536]{1,0:T(8,128)} fusion(bf16[1024,768]{1,0:T(8,128)(2,1)} %all-gather.6.cloned.1.call-done, bf16[1536,768]{1,0:T(8,128)(2,1)S(1)} %copy-done), kind=kOutput, calls=%fused_computation.22 | convolution fusion | flops 2415919104 | bytes 10223616 | tf_op jit(solution)/shard_map/dot_general | solution.py:25
  167.8 0.0 reduce-scatter.5.cloned.1.call-update
  167.8 6.7 %convolution_convert_fusion = bf16[768,1536]{1,0:T(8,128)(2,1)} fusion(bf16[1024,1536]{1,0:T(8,128)(2,1)} %all-gather.4.cloned.1.call-done, bf16[1024,768]{1,0:T(8,128)(2,1)} %param.6), kind=kOutput, calls=%fused_computation.1 | convolution fusion | flops 2424963072 | bytes 7077888 | tf_op jit(solution)/shard_map/dot_general | solution.py:19
  174.5 71.0 %all-gather.8.cloned.1.call-done = bf16[1024,1536]{1,0:T(8,128)(2,1)} async-done(((bf16[32,1536]{1,0:T(8,128)(2,1)}), bf16[1024,1536]{1,0:T(8,128)(2,1)}) %all-gather.8.cloned.1.call-update) | async-done | bytes 3145744 | tf_op jit(solution)/shard_map/all_gather | solution.py:35
  245.5 6.5 %fusion.2 = bf16[1536,768]{0,1:T(8,128)(2,1)} fusion(bf16[1024,768]{1,0:T(8,128)(2,1)} %all-gather.6.cloned.1.call-done, bf16[1024,1536]{1,0:T(8,128)(2,1)} %all-gather.8.cloned.1.call-done), kind=kOutput, calls=%fused_computation.6 | convolution fusion | flops 2417098752 | bytes 7077888 | tf_op jit(solution)/shard_map/dot_general | solution.py:19
  252.0 4.3 copy.8
  256.3 216.7 %reduce-scatter.5.cloned.1.call-done = f32[32,1536]{1,0:T(8,128)} async-done(((f32[1024,1536]{1,0:T(8,128)}), f32[32,1536]{1,0:T(8,128)}) %reduce-scatter.5.cloned.1.call-update) | async-done | bytes 196624 | tf_op jit(solution)/shard_map/reduce_scatter | solution.py:47
  473.0 1.6 convert_element_type.23
Async XLA Ops:
  7.2 154.6 %copy-start = (bf16[1536,768]{1,0:T(8,128)(2,1)S(1)}, bf16[1536,768]{1,0:T(8,128)(2,1)}, u32[]{:S(2)}) copy-start(bf16[1536,768]{1,0:T(8,128)(2,1)} %param.8) | copy-start | bytes 7077892
  7.2 85.8 %all-gather.4.cloned.1.call-start = ((), (), s32[]{:S(2)}) async-start(), calls=%async_computation.2 | async-start | bytes 3244032 | tf_op jit(solution)/shard_map/all_gather | solution.py:34
  7.9 124.0 %reduce-scatter.3.cloned.1.call-start = ((), (), s32[]{:S(2)}) async-start(), calls=%async_computation.3 | async-start | bytes 3538944 | tf_op jit(solution)/shard_map/reduce_scatter | solution.py:40
  99.9 61.9 %all-gather.6.cloned.1.call-start = ((), (), s32[]{:S(2)}) async-start(), calls=%async_computation.4 | async-start | bytes 1769472 | tf_op jit(solution)/shard_map/all_gather | solution.py:45
  134.2 111.3 %all-gather.8.cloned.1.call-start = ((), (), s32[]{:S(2)}) async-start(), calls=%async_computation.6 | async-start | bytes 3244032 | tf_op jit(solution)/shard_map/all_gather | solution.py:35
  134.8 338.2 %reduce-scatter.5.cloned.1.call-start = ((), (), s32[]{:S(2)}) async-start(), calls=%async_computation.5 | async-start | bytes 6488064 | tf_op jit(solution)/shard_map/reduce_scatter | solution.py:47
Sparse Core Ops, SparseCore 0:
  10.6 82.4 all-gather.3
  100.0 31.7 reduce-scatter.2
  134.3 27.4 all-gather.5
  164.2 81.2 all-gather.7
  249.3 223.5 reduce-scatter.4
where the time goes:
time: 481 us
  waiting for transfers between devices  424 us (88%)
  matrix products  26.1 us (5%)
  between operations  13.8 us (3%)
  other arithmetic  13.1 us (3%)
    reduce_scatter x1, waiting for transfers between devices, body(): lax.psum_scatter(contract_cols(piece, weight_in), 'row', scatter_dimensio...  217 us
    all_gather x1, waiting for transfers between devices, body(): lax.all_gather(out_grad, 'row', axis=0, tiled=True)  85.1 us
    all_gather x1, waiting for transfers between devices, body(): lax.all_gather(inputs, 'row', axis=0, tiled=True)  71 us
    all_gather x1, waiting for transfers between devices, body(): d_hid = lax.all_gather(d_mine, 'col', axis=0, tiled=True)  27 us
    reduce_scatter x1, waiting for transfers between devices, body(): lax.psum_scatter(contract_cols(piece, weight_out), 'col', scatter_dimensi...  22.6 us
    dot_general x2, matrix products, contract_rows(): lax.dot_general(left, right, (((0,), (0,)), ((), ())), preferred_element_...  13.2 us
    dot_general x2, matrix products, contract_cols(): lax.dot_general(left, right, (((1,), (1,)), ((), ())), preferred_element_...  12.9 us
  transfers between devices with their start and end apart: 5, of which 5 were waited for; matrix products, arithmetic and copies ran while one was open for 7% of the time, Pallas kernels for 0%

commit v1 on v0

--- a/solution.py
+++ b/solution.py
@@ -2,6 +2,13 @@
 import jax.numpy as jnp
 from jax import lax
 from jax.sharding import PartitionSpec as P
+
+
+def swapped_in(block, axis, dim):
+    n_dev = lax.axis_size(axis)
+    blocks = jnp.stack([block for _ in range(n_dev)])
+    blocks = lax.all_to_all(blocks, axis, split_axis=0, concat_axis=0)
+    return jnp.concatenate(blocks, axis=dim)
 
 
 def gelu_parts(hidden_pre):
@@ -32,7 +39,7 @@
     act_b = act.astype(jnp.bfloat16)
     grad_all, input_all = (
         lax.all_gather(out_grad, "row", axis=0, tiled=True),
-        lax.all_gather(inputs, "row", axis=0, tiled=True),
+        swapped_in(inputs, "row", 0),
     )
     grad_weight_out = contract_rows(act_b, grad_all).astype(jnp.bfloat16)
     col_rows = grad_all.shape[0] // lax.axis_size("col")

time: 481 us -> 434 us (0.902)
  waiting for transfers between devices: 424 us -> 364 us
  starting transfers between devices: 0.2 us -> 10.1 us
    all_to_all x0 -> x1, waiting for transfers between devices: none -> 83.1 us  [swapped_in(): blocks = lax.all_to_all(blocks, axis, split_axis=0, concat_axis=0)]
    reduce_scatter x1, waiting for transfers between devices: 217 us -> 144 us  [body(): lax.psum_scatter(contract_cols(piece, weight_in), 'row', scatter_dimensio...]
    all_gather x1 -> x0, waiting for transfers between devices: 71 us -> none  [body(): lax.all_gather(inputs, 'row', axis=0, tiled=True)]
    all_to_all x0 -> x1, starting transfers between devices: none -> 9.97 us  [swapped_in(): blocks = lax.all_to_all(blocks, axis, split_axis=0, concat_axis=0)]
where the time goes in v1:
time: 434 us
  waiting for transfers between devices  364 us (84%)
  matrix products  26.2 us (6%)
  between operations  13.8 us (3%)
  other arithmetic  13.1 us (3%)
  starting transfers between devices  10.1 us (2%)
  local copies, waits for them, and re-layouts  7.13 us (2%)
    reduce_scatter x1, waiting for transfers between devices, body(): lax.psum_scatter(contract_cols(piece, weight_in), 'row', scatter_dimensio...  144 us
    all_gather x1, waiting for transfers between devices, body(): lax.all_gather(out_grad, 'row', axis=0, tiled=True)  85.1 us
    all_to_all x1, waiting for transfers between devices, swapped_in(): blocks = lax.all_to_all(blocks, axis, split_axis=0, concat_axis=0)  83.1 us
    all_gather x1, waiting for transfers between devices, body(): d_hid = lax.all_gather(d_mine, 'col', axis=0, tiled=True)  27.6 us
    reduce_scatter x1, waiting for transfers between devices, body(): lax.psum_scatter(contract_cols(piece, weight_out), 'col', scatter_dimensi...  22.6 us
    dot_general x2, matrix products, contract_rows(): lax.dot_general(left, right, (((0,), (0,)), ((), ())), preferred_element_...  13.4 us
    dot_general x2, matrix products, contract_cols(): lax.dot_general(left, right, (((1,), (1,)), ((), ())), preferred_element_...  12.9 us
    all_to_all x1, starting transfers between devices, swapped_in(): blocks = lax.all_to_all(blocks, axis, split_axis=0, concat_axis=0)  9.97 us
  transfers between devices with their start and end apart: 5, of which 5 were waited for; matrix products, arithmetic and copies ran while one was open for 7% of the time, Pallas kernels for 0%

profile of v1, /device:TPU:2, one launch (start us, length us, event | category | flops | bytes accessed | tf_op | source)
XLA Modules:
  0.0 434.0 jit_solution(12248637358237895837)
XLA Ops:
  7.2 0.0 copy-start
  7.2 0.0 all-gather.3.cloned.1.call-start
  7.2 0.7 all-gather.3.cloned.1.call-update
  7.9 0.0 reduce-scatter.3.cloned.1.call-start
  8.0 85.1 %all-gather.3.cloned.1.call-done = bf16[1024,1536]{1,0:T(8,128)(2,1)} async-done(((bf16[32,1536]{1,0:T(8,128)(2,1)}), bf16[1024,1536]{1,0:T(8,128)(2,1)}) %all-gather.3.cloned.1.call-update) | async-done | bytes 3145744 | tf_op jit(solution)/shard_map/all_gather | solution.py:41
  93.0 6.9 %fusion.12 = f32[1024,768]{1,0:T(8,128)} fusion(bf16[1024,1536]{1,0:T(8,128)(2,1)} %all-gather.3.cloned.1.call-done, bf16[768,1536]{1,0:T(8,128)(2,1)} %param.9), kind=kOutput, calls=%fused_computation.21 | convolution fusion | flops 2415919104 | bytes 8650752 | tf_op jit(solution)/shard_map/dot_general | solution.py:32
  99.9 0.0 reduce-scatter.3.cloned.1.call-update
  99.9 0.0 all-gather.5.cloned.1.call-start
  100.0 3.3 convert_element_type.21
  103.3 6.0 %fusion.1 = (f32[1024,768]{1,0:T(8,128)}, f32[1024,768]{1,0:T(8,128)}, f32[1024,768]{1,0:T(8,128)}) fusion(bf16[1024,768]{1,0:T(8,128)(2,1)} %param.6), kind=kLoop, calls=%fused_computation.4 | loop fusion | flops 6291456 | bytes 11010048 | tf_op jit(solution)/shard_map/tanh | solution.py:17
  109.2 22.6 %reduce-scatter.3.cloned.1.call-done = f32[128,768]{1,0:T(8,128)} async-done(((f32[1024,768]{1,0:T(8,128)}), f32[128,768]{1,0:T(8,128)}) %reduce-scatter.3.cloned.1.call-update) | async-done | bytes 393232 | tf_op jit(solution)/shard_map/reduce_scatter | solution.py:47
  131.9 2.3 fusion.7
  134.2 0.0 all-gather.5.cloned.1.call-update
  134.2 0.0 reduce-scatter.5.cloned.1.call-start
  134.3 27.6 %all-gather.5.cloned.1.call-done = bf16[1024,768]{1,0:T(8,128)(2,1)} async-done(((bf16[128,768]{1,0:T(8,128)(2,1)}), bf16[1024,768]{1,0:T(8,128)(2,1)}) %all-gather.5.cloned.1.call-update) | async-done | bytes 1572880 | tf_op jit(solution)/shard_map/all_gather | solution.py:52
  161.8 0.0 copy-done
  161.8 6.0 %fusion.13 = f32[1024,1536]{1,0:T(8,128)} fusion(bf16[1024,768]{1,0:T(8,128)(2,1)} %all-gather.5.cloned.1.call-done, bf16[1536,768]{1,0:T(8,128)(2,1)S(1)} %copy-done), kind=kOutput, calls=%fused_computation.22 | convolution fusion | flops 2415919104 | bytes 10223616 | tf_op jit(solution)/shard_map/dot_general | solution.py:32
  167.8 0.0 copy-start.1
  167.8 0.0 reduce-scatter.5.cloned.1.call-update
  167.8 0.9 copy-done.1
  168.7 2.0 stack.2
  170.7 10.0 %all-to-all-start = ((bf16[32,32,1536]{2,1,0:T(8,128)(2,1)}), bf16[32,32,1536]{2,1,0:T(8,128)(2,1)}, u32[]{:S(2)}, u32[]{:S(2)}) async-start(bf16[32,32,1536]{2,1,0:T(8,128)(2,1)} %stack.2), calls=%async_computation.2 | async-start | bytes 6291456 | tf_op jit(solution)/shard_map/all_to_all | solution.py:10
  180.6 6.9 %convolution_convert_fusion = bf16[768,1536]{1,0:T(8,128)(2,1)} fusion(bf16[1024,1536]{1,0:T(8,128)(2,1)} %all-gather.3.cloned.1.call-done, bf16[1024,768]{1,0:T(8,128)(2,1)} %param.6), kind=kOutput, calls=%fused_computation.1 | convolution fusion | flops 2424963072 | bytes 7077888 | tf_op jit(solution)/shard_map/dot_general | solution.py:26
  187.5 83.1 %all-to-all-done = bf16[32,32,1536]{2,1,0:T(8,128)(2,1)} async-done(((bf16[32,32,1536]{2,1,0:T(8,128)(2,1)}), bf16[32,32,1536]{2,1,0:T(8,128)(2,1)}, u32[]{:S(2)}, u32[]{:S(2)}) %all-to-all-start) | async-done | bytes 3145760 | tf_op jit(solution)/shard_map/all_to_all | solution.py:10
  270.6 6.5 %fusion.2 = bf16[1536,768]{0,1:T(8,128)(2,1)} fusion(bf16[1024,768]{1,0:T(8,128)(2,1)} %all-gather.5.cloned.1.call-done, bf16[1024,1536]{1,0:T(8,128)(2,1)} %bitcast), kind=kOutput, calls=%fused_computation.6 | convolution fusion | flops 2417098752 | bytes 7077888 | tf_op jit(solution)/shard_map/dot_general | solution.py:26
  277.1 4.3 copy.8
  281.4 144.5 %reduce-scatter.5.cloned.1.call-done = f32[32,1536]{1,0:T(8,128)} async-done(((f32[1024,1536]{1,0:T(8,128)}), f32[32,1536]{1,0:T(8,128)}) %reduce-scatter.5.cloned.1.call-update) | async-done | bytes 196624 | tf_op jit(solution)/shard_map/reduce_scatter | solution.py:54
  425.9 1.6 convert_element_type.23
Async XLA Ops:
  7.2 154.6 %copy-start = (bf16[1536,768]{1,0:T(8,128)(2,1)S(1)}, bf16[1536,768]{1,0:T(8,128)(2,1)}, u32[]{:S(2)}) copy-start(bf16[1536,768]{1,0:T(8,128)(2,1)} %param.8) | copy-start | bytes 7077892
  7.2 85.8 %all-gather.3.cloned.1.call-start = ((), (), s32[]{:S(2)}) async-start(), calls=%async_computation.3 | async-start | bytes 3244032 | tf_op jit(solution)/shard_map/all_gather | solution.py:41
  7.9 124.0 %reduce-scatter.3.cloned.1.call-start = ((), (), s32[]{:S(2)}) async-start(), calls=%async_computation.4 | async-start | bytes 3538944 | tf_op jit(solution)/shard_map/reduce_scatter | solution.py:47
  99.9 61.9 %all-gather.5.cloned.1.call-start = ((), (), s32[]{:S(2)}) async-start(), calls=%async_computation.5 | async-start | bytes 1769472 | tf_op jit(solution)/shard_map/all_gather | solution.py:52
  134.2 291.7 %reduce-scatter.5.cloned.1.call-start = ((), (), s32[]{:S(2)}) async-start(), calls=%async_computation.6 | async-start | bytes 6488064 | tf_op jit(solution)/shard_map/reduce_scatter | solution.py:54
  167.8 0.9 copy-start.1
  170.7 100.0 %all-to-all-start = ((bf16[32,32,1536]{2,1,0:T(8,128)(2,1)}), bf16[32,32,1536]{2,1,0:T(8,128)(2,1)}, u32[]{:S(2)}, u32[]{:S(2)}) async-start(bf16[32,32,1536]{2,1,0:T(8,128)(2,1)} %stack.2), calls=%async_computation.2 | async-start | bytes 6291456 | tf_op jit(solution)/shard_map/all_to_all | solution.py:10
Sparse Core Ops, SparseCore 0:
  10.6 82.4 all-gather.2
  100.0 31.7 reduce-scatter.2
  134.3 27.4 all-gather.4
  167.9 257.8 reduce-scatter.4
